TPU v7x, 128 devices: a whole 4x4x4 slice. The times are simulated.
128 devices in a mesh: dp: 4 (over y), expert: 32 (over z, x, core).
Axes of the slice: x: 4, y: 4, z: 4, core: 2. Of those that a mesh axis runs over, the one named last changes fastest.
Arguments:
- tokens: bfloat16 [16384, 2048], P(('dp', 'expert')), may hold values from -6 to 6
- expert_ids: int32 [16384, 8], P(('dp', 'expert')), may hold values from 0 to 63, all different within a row
- bucket_codes: int32 [16384, 8], P(('dp', 'expert')), may hold values from 0 to 65535
- route_weights: float32 [16384, 8], P(('dp', 'expert')), may hold values from 0.1 to 1
- cotangent: bfloat16 [16384, 2048], P(('dp', 'expert')), may hold values from -2 to 2
- counts: int32 [64], replicated, may hold values from 4 to 16, as said below
- comp_scale: bfloat16 [64, 2048], replicated, may hold values from -3 to 3
- w_gate: bfloat16 [64, 2048, 768], P('expert'), may hold values from -0.125 to 0.125
- w_up: bfloat16 [64, 2048, 768], P('expert'), may hold values from -0.125 to 0.125
- w_down: bfloat16 [64, 768, 2048], P('expert'), may hold values from -0.21875 to 0.21875
Outputs:
- layer_output: bfloat16 [16384, 2048], P(('dp', 'expert'))
- grad_tokens: bfloat16 [16384, 2048], P(('dp', 'expert'))
- grad_down: bfloat16 [64, 768, 2048], P('expert', None, 'dp')
Inputs may be any that keep to these rules, and one draw needn't show every extreme that they name: `counts`: experts 2i and 2i+1 (those of index i of the expert axis) have 20 buckets together; some expert has exactly 16. `expert_ids`: the 8 experts of one token differ.
All inputs are finite; a program needn't handle non-finite values.
Results may differ from a plain program's by a relative error of at most 0.013.
Values may be sent and summed in bfloat16 or wider, within the bound.
A program may use at most 192 MiB of HBM per device.

v0:
```python
import functools

import jax
import jax.numpy as jnp
from jax import lax
from jax.experimental import pallas as pl
from jax.experimental.pallas import tpu as pltpu
from jax.sharding import PartitionSpec as P

MESH = pl.DeviceIdType.MESH
F32 = jnp.float32
BF16 = jnp.bfloat16
NZ, NX, NC, NY = 4, 4, 2, 4
PAIR = 20
TOP = 16
REST = PAIR - TOP
LINE = 4 * PAIR
LANES = 128
FAR = (2, 1, 3, 0)


def dot(a, b, ca=1, cb=0):
    return lax.dot_general(a, b, (((ca,), (cb,)), ((), ())), preferred_element_type=F32)


def kernel(
    counts_ref, ids_ref, codes_ref, route_ref, tok_ref, cot_ref, comp_ref, wg_hbm, wu_hbm, wd_hbm,
    layer_ref, grad_ref, down_hbm, mid_a0, mid_a1, mid_b0, mid_b1, mid_c0, mid_c1, mid_d0, mid_d1,
    send_0, send_1, got_a, got_b, got_c, got_d, wg, wu, wd, rows, gate, up, hid, dgs, dus,
    part, relay, final, mix_out, mix_in, loc_out, loc_in, wsem, osem, ss1, rs1, ss2, rs2, yss, yrs,
):
    devs = NZ * NX * NC
    top_rows, all_rows = devs * TOP, devs * PAIR
    tok_n, width = tok_ref.shape
    quarter = width // 4
    ff = wg.shape[2]
    me, y = lax.axis_index("expert"), lax.axis_index("dp")
    c, x, z = me % NC, (me // NC) % NX, me // (NC * NX)

    def at(zz, xx, cc):
        return {"expert": (zz * NX + xx) * NC + cc}

    def x_dev(dx, dc, back=False):
        return at(z, (x + (NX - dx if back else dx)) % NX, (c + dc) % NC)

    def z_dev(dz, dc, back=False):
        return at((z + (NZ - dz if back else dz)) % NZ, x, (c + dc) % NC)

    def y_dev(dy):
        return {"dp": (y + dy) % NY}

    peers = [x_dev(d, k) for d in range(NX) for k in range(NC) if d + k]
    peers += [z_dev(d, k) for d in range(1, NZ) for k in range(NC)]
    peers += [y_dev(1), y_dev(NY - 1)]
    barrier = pltpu.get_barrier_semaphore()
    for peer in peers:
        pl.semaphore_signal(barrier, inc=1, device_id=peer, device_id_type=MESH)

    loads = [
        pltpu.make_async_copy(src, dst, wsem.at[i])
        for i, (src, dst) in enumerate(((wg_hbm, wg), (wu_hbm, wu), (wd_hbm, wd)))
    ]
    for load in loads:
        load.start()

    sends = (send_0, send_1, send_0, send_1)
    mids = ((mid_a0, mid_a1), (mid_b0, mid_b1), (mid_c0, mid_c1), (mid_d0, mid_d1))
    gots = (got_a, got_b, got_c, got_d)

    def copies(n, phase):
        out = ([], [])
        buf, (mid_x, mid_z), got = sends[n], mids[n], gots[n]
        ssem, rsem = ((ss1, rs1), (ss2, rs2))[phase]
        for d in FAR:
            for k in (1, 0):
                cc = (c + k) % NC
                xx, zz = (x + d) % NX, (z + d) % NZ
                if phase == 0:
                    moves = (
                        (buf.at[cc, :, xx], mid_x.at[x, c], x_dev(d, k)),
                        (buf.at[NC + cc, zz], mid_z.at[z, c], z_dev(d, k)),
                    )
                else:
                    moves = (
                        (mid_z.at[:, :, xx, cc], got.at[NC + c, :, x], x_dev(d, k)),
                        (mid_x.at[:, :, zz, cc], got.at[c, z], z_dev(d, k)),
                    )
                for side, (src, dst, dev) in enumerate(moves):
                    i = d * NC + k
                    if d + k:
                        out[side].append(functools.partial(
                            pltpu.make_async_remote_copy, src_ref=src, dst_ref=dst,
                            send_sem=ssem.at[n, side, i], recv_sem=rsem.at[n, side, i],
                            device_id=dev, device_id_type=MESH,
                        ))
                    else:
                        out[side].append(functools.partial(
                            pltpu.make_async_copy, src, dst, rsem.at[n, side, i]
                        ))
        return out

    def start(n, phase, sides=(0, 1)):
        both = copies(n, phase)
        for i in range(len(both[0])):
            for side in sides:
                both[side][i]().start()

    def arrive(n, phase, sides=(0, 1)):
        both = copies(n, phase)
        for side in sides:
            for copy in both[side][:-1]:
                copy().wait_recv()
            both[side][-1]().wait()

    def sent(n, phase):
        for side in copies(n, phase):
            for copy in side[:-1]:
                copy().wait_send()

    def relay_on(n):
        arrive(n, 0, (0,))
        start(n, 1, (1,))
        arrive(n, 0, (1,))
        start(n, 1, (0,))

    def pick(q, rows_n, cols_n, flip):
        i = lax.broadcasted_iota(jnp.int32, (rows_n, cols_n), 1 if flip else 0)
        j = lax.broadcasted_iota(jnp.int32, (rows_n, cols_n), 0 if flip else 1)
        return (j == (i // REST) * TOP + q * REST + i % REST).astype(F32).astype(BF16)

    def put_rows(n, q, value):
        buf = sends[n]
        rest = dot(pick(q, top_rows, devs * REST, True), value[top_rows:])
        line = lax.broadcasted_iota(jnp.int32, (top_rows, 1), 0) % TOP // REST
        at_q = pl.ds(pl.multiple_of(q * TOP, TOP), TOP)
        for g in range(4):
            cut = slice(g * LANES, (g + 1) * LANES)
            buf[g, :, :, :, at_q, :] = value[:top_rows, cut].reshape(NZ, NX, NC, TOP, LANES)
            old = buf[g, :, :, :, 4 * TOP:, :].reshape(top_rows, LANES)
            new = jnp.where(line == q, rest[:, cut], old.astype(F32)).astype(BF16)
            buf[g, :, :, :, 4 * TOP:, :] = new.reshape(NZ, NX, NC, TOP, LANES)

    def take_rows(n):
        got = gots[n]

        def body(q, carry):
            at_q = pl.ds(pl.multiple_of(q * TOP, TOP), TOP)
            col = pl.multiple_of(q * quarter, quarter)
            sel = pick(q, devs * REST, top_rows, False)
            for g in range(4):
                lanes = pl.ds(pl.multiple_of(col + g * LANES, LANES), LANES)
                rows[:top_rows, lanes] = got[g, :, :, :, at_q, :].reshape(top_rows, LANES)
            rest = jnp.concatenate(
                [got[g, :, :, :, 4 * TOP:, :].reshape(top_rows, LANES) for g in range(4)], axis=1
            )
            rows[top_rows:, pl.ds(col, quarter)] = dot(sel, rest).astype(BF16)
            return carry

        lax.fori_loop(0, 4, body, 0)

    ids, codes, route = ids_ref[...], codes_ref[...], route_ref[...]
    experts = 2 * devs
    size = jnp.ones_like(ids)
    base = jnp.zeros_like(ids)
    for e in range(experts):
        hit = ids == e
        size = jnp.where(hit, counts_ref[e], size)
        if e % 2:
            base = jnp.where(hit, counts_ref[e - 1], base)
    code_f, size_f = codes.astype(F32), size.astype(F32)
    bucket = base + codes - jnp.floor((code_f + 0.5) / size_f).astype(jnp.int32) * size
    dest = ids // 2
    row_id = jnp.where(bucket < TOP, dest * TOP + bucket, top_rows + dest * REST + bucket - TOP)
    row_iota = lax.broadcasted_iota(jnp.int32, (all_rows, tok_n), 0)
    member = jnp.zeros((all_rows, tok_n), F32)
    weight = jnp.zeros((all_rows, tok_n), F32)
    e_iota = lax.broadcasted_iota(jnp.int32, (experts, tok_n), 0)
    gain = jnp.zeros((experts, tok_n), F32)
    for k in range(ids.shape[0]):
        hit = row_iota == row_id[k:k + 1, :]
        member = jnp.where(hit, 1.0, member)
        weight = jnp.where(hit, route[k:k + 1, :], weight)
        gain = jnp.where(e_iota == ids[k:k + 1, :], route[k:k + 1, :], gain)
    inverse = 1.0 / jnp.maximum(jnp.sum(member, axis=1, keepdims=True), 1.0)
    member_b, weight_b = member.astype(BF16), weight.astype(BF16)
    mix_out[...] = weight.T.astype(BF16)
    mix_in[...] = (member * inverse).T.astype(BF16)
    gain_b = gain.T.astype(BF16)

    row_e = lax.broadcasted_iota(jnp.int32, (all_rows, experts), 0)
    col_e = lax.broadcasted_iota(jnp.int32, (all_rows, experts), 1)
    row_dest = jnp.where(row_e < top_rows, row_e // TOP, (row_e - top_rows) // REST)
    row_bucket = jnp.where(row_e < top_rows, row_e % TOP, TOP)
    first = lax.broadcasted_iota(jnp.int32, (1, experts), 1)
    first_n = jnp.zeros((1, experts), jnp.int32)
    for j in range(devs):
        first_n = jnp.where(first // 2 == j, counts_ref[2 * j], first_n)
    owner = jnp.where(
        (col_e // 2 == row_dest) & ((row_bucket >= first_n) == (col_e % 2 == 1)), 1.0, 0.0
    ).astype(BF16)

    def head(n, lhs, scale, src, mix, loc):
        def sums(q, carry):
            cols = pl.ds(pl.multiple_of(q * quarter, quarter), quarter)
            value = dot(lhs, src[:, cols])
            if scale is not None:
                value = value * scale
            value = value.astype(BF16)
            rows[:, cols] = value
            put_rows(n, q, value)
            return carry

        lax.fori_loop(0, 4, sums, 0)
        if n == 0:
            pl.semaphore_wait(barrier, len(peers))
        start(n, 0)

        def local(q, carry):
            cols = pl.ds(pl.multiple_of(q * quarter, quarter), quarter)
            comp = comp_ref[:, cols]
            scaled = (dot(owner, comp) * rows[:, cols].astype(F32)).astype(BF16)
            loc[:, cols] = dot(gain_b, comp) * src[:, cols].astype(F32) - dot(mix[...], scaled)
            return carry

        lax.fori_loop(0, 4, local, 0)

    for ref in (send_0, send_1):
        ref[:, :, :, :, 4 * TOP:, :] = jnp.zeros((4, NZ, NX, NC, TOP, LANES), BF16)
    head(0, member_b, inverse, tok_ref, mix_out, loc_out)
    head(1, weight_b, None, cot_ref, mix_in, loc_in)
    relay_on(0)
    relay_on(1)
    sent(0, 0)
    for load in loads:
        load.wait()

    mine = counts_ref[2 * me]
    row_1 = lax.broadcasted_iota(jnp.int32, (all_rows, 1), 0)
    zero_exp = (row_1 < top_rows) & (row_1 % TOP < mine)
    step = 256
    arrive(0, 1)
    take_rows(0)

    def both(w, cols):
        return jnp.where(zero_exp, dot(rows[...], w[0, :, cols]), dot(rows[...], w[1, :, cols]))

    def split(ref, f, value):
        ref[:, pl.ds(f, step)] = jnp.where(zero_exp, value, 0.0).astype(BF16)
        ref[:, pl.ds(pl.multiple_of(f + ff, step), step)] = jnp.where(zero_exp, 0.0, value).astype(BF16)

    def forward(i, carry):
        f = pl.multiple_of(i * step, step)
        cols = pl.ds(f, step)
        g, u = both(wg, cols), both(wu, cols)
        gate[:, cols] = g.astype(BF16)
        up[:, cols] = u.astype(BF16)
        split(hid, f, g * jax.nn.sigmoid(g) * u)
        return carry

    lax.fori_loop(0, ff // step, forward, 0)

    def out_cols(q, carry):
        cols = pl.ds(pl.multiple_of(q * quarter, quarter), quarter)
        put_rows(2, q, dot(hid[...], wd[:, cols]).astype(BF16))
        return carry

    lax.fori_loop(0, 4, out_cols, 0)
    start(2, 0)

    arrive(1, 1)
    sent(1, 0)
    take_rows(1)

    def y_copy(i):
        e, dest, sign, dst = (
            (0, 2, 1, relay.at[0]), (1, 2, NY - 1, relay.at[1]),
            (1, 1, 1, final.at[0, 1]), (0, NY - 1, NY - 1, final.at[1, 0]),
            (0, 1, 1, final.at[0, 0]), (1, NY - 1, NY - 1, final.at[1, 1]),
        )[i]
        return pltpu.make_async_remote_copy(
            src_ref=part.at[(y + dest) % NY, e], dst_ref=dst, send_sem=yss.at[i],
            recv_sem=yrs.at[i], device_id=y_dev(sign), device_id_type=MESH,
        )

    def down(shift):
        owner_y = (y + shift) % NY
        cols = pl.ds(pl.multiple_of(owner_y * quarter, quarter), quarter)

        def body(i, carry):
            f = pl.multiple_of(i * step, step)
            for e in range(2):
                at_f = pl.ds(pl.multiple_of(f + e * ff, step), step)
                part[owner_y, e, pl.ds(f, step), :] = dot(hid[:, at_f], rows[:, cols], 0, 0).astype(BF16)
            return carry

        lax.fori_loop(0, ff // step, body, 0)

    down(2)
    y_copy(0).start()
    y_copy(1).start()
    down(1)
    y_copy(2).start()
    down(NY - 1)
    y_copy(3).start()
    down(0)

    def backward(i, carry):
        f = pl.multiple_of(i * step, step)
        cols = pl.ds(f, step)
        high = pl.ds(pl.multiple_of(f + ff, step), step)
        dh = jnp.where(zero_exp, dot(rows[...], wd[cols, :], 1, 1), dot(rows[...], wd[high, :], 1, 1))
        g, u = gate[:, cols].astype(F32), up[:, cols].astype(F32)
        s = jax.nn.sigmoid(g)
        split(dgs, f, dh * u * s * (1.0 + g * (1.0 - s)))
        split(dus, f, dh * g * s)
        return carry

    lax.fori_loop(0, ff // step, backward, 0)
    relay_on(2)

    def back_cols(q, carry):
        at_q = pl.ds(pl.multiple_of(q * quarter, quarter), quarter)
        total = jnp.zeros((all_rows, quarter), F32)
        for e in range(2):
            half = slice(e * ff, (e + 1) * ff)
            total += dot(dgs[:, half], wg[e, at_q, :], 1, 1)
            total += dot(dus[:, half], wu[e, at_q, :], 1, 1)
        put_rows(3, q, total.astype(BF16))
        return carry

    lax.fori_loop(0, 4, back_cols, 0)
    start(3, 0)

    for i, shift, e in ((0, 1, 0), (1, NY - 1, 1)):
        y_copy(i).wait_recv()
        owner_y = (y + shift) % NY

        def add(j, carry):
            at_f = pl.ds(pl.multiple_of(j * step, step), step)
            total = part[owner_y, e, at_f, :].astype(F32) + relay[i, at_f, :].astype(F32)
            part[owner_y, e, at_f, :] = total.astype(BF16)
            return carry

        lax.fori_loop(0, ff // step, add, 0)
        y_copy(4 + i).start()
    relay_on(3)

    def tail(n, mix, loc, out_ref):
        arrive(n, 1)
        take_rows(n)

        def body(q, carry):
            cols = pl.ds(pl.multiple_of(q * quarter, quarter), quarter)
            out_ref[:, cols] = (loc[:, cols] + dot(mix[...], rows[:, cols])).astype(BF16)
            return carry

        lax.fori_loop(0, 4, body, 0)

    tail(2, mix_out, loc_out, layer_ref)
    for i in range(2, 6):
        y_copy(i).wait_recv()

    def finish(j, carry):
        at_f = pl.ds(pl.multiple_of(j * step, step), step)
        for e in range(2):
            total = part[y, e, at_f, :].astype(F32) + final[0, e, at_f, :].astype(F32)
            relay[e, at_f, :] = (total + final[1, e, at_f, :].astype(F32)).astype(BF16)
        return carry

    lax.fori_loop(0, ff // step, finish, 0)
    down_out = pltpu.make_async_copy(relay, down_hbm, osem)
    down_out.start()
    tail(3, mix_in, loc_in, grad_ref)
    for n in range(4):
        if n >= 2:
            sent(n, 0)
        sent(n, 1)
    for i in range(6):
        y_copy(i).wait_send()
    down_out.wait()


def on_device(
    tokens, expert_ids, bucket_codes, route_weights, cotangent, counts, comp_scale, w_gate, w_up, w_down
):
    tok_n, width = tokens.shape
    local, _, ff = w_gate.shape
    devs = NZ * NX * NC
    all_rows, quarter = devs * PAIR, width // 4
    vmem = pl.BlockSpec(memory_space=pltpu.VMEM)
    hbm = pl.BlockSpec(memory_space=pl.ANY)
    mid = jax.ShapeDtypeStruct((4, NC, 4, NC, LINE, LANES), BF16)
    rows_buf = pltpu.VMEM((4, NZ, NX, NC, LINE, LANES), BF16)
    dma = pltpu.SemaphoreType.DMA
    out = pl.pallas_call(
        kernel,
        out_shape=[
            jax.ShapeDtypeStruct((tok_n, width), BF16),
            jax.ShapeDtypeStruct((tok_n, width), BF16),
            jax.ShapeDtypeStruct((local, ff, quarter), BF16),
        ] + [mid] * 8,
        in_specs=[pl.BlockSpec(memory_space=pltpu.SMEM)] + [vmem] * 6 + [hbm] * 3,
        out_specs=[vmem] * 2 + [hbm] * 9,
        scratch_shapes=[rows_buf] * 6 + [
            pltpu.VMEM((local, width, ff), BF16),
            pltpu.VMEM((local, width, ff), BF16),
            pltpu.VMEM((local * ff, width), BF16),
            pltpu.VMEM((all_rows, width), BF16),
            pltpu.VMEM((all_rows, ff), BF16),
            pltpu.VMEM((all_rows, ff), BF16),
            pltpu.VMEM((all_rows, local * ff), BF16),
            pltpu.VMEM((all_rows, local * ff), BF16),
            pltpu.VMEM((all_rows, local * ff), BF16),
            pltpu.VMEM((NY, local, ff, quarter), BF16),
            pltpu.VMEM((2, ff, quarter), BF16),
            pltpu.VMEM((2, local, ff, quarter), BF16),
            pltpu.VMEM((tok_n, all_rows), BF16),
            pltpu.VMEM((tok_n, all_rows), BF16),
            pltpu.VMEM((tok_n, width), F32),
            pltpu.VMEM((tok_n, width), F32),
            dma((3,)), dma, dma((4, 2, 8)), dma((4, 2, 8)), dma((4, 2, 8)), dma((4, 2, 8)),
            dma((6,)), dma((6,)),
        ],
        compiler_params=pltpu.CompilerParams(
            collective_id=0, has_side_effects=True, vmem_limit_bytes=67043328
        ),
    )(
        counts, expert_ids.T, bucket_codes.T, route_weights.T, tokens, cotangent, comp_scale,
        w_gate, w_up, w_down.reshape(local * ff, width),
    )
    return tuple(out[:3])


def solution(mesh):
    rows = P(("dp", "expert"), None)
    stack = P("expert", None, None)
    return jax.shard_map(
        on_device,
        mesh=mesh,
        in_specs=(rows, rows, rows, rows, rows, P(), P(), stack, stack, stack),
        out_specs=(rows, rows, P("expert", None, "dp")),
        check_vma=False,
    )
```

profile of v0, /device:TPU:1, one launch (start us, length us, event | category | flops | bytes accessed | tf_op | source)
XLA Modules:
  0.0 145.2 jit_solution(2984295290311080618)
XLA Ops:
  0.6 139.6 %shard_map.121 = (bf16[128,2048]{1,0:T(8,128)(2,1)}, bf16[128,2048]{1,0:T(8,128)(2,1)}, bf16[2,768,512]{2,1,0:T(8,128)(2,1)}, bf16[4,2,4,2,80,128]{5,4,3,2,1,0:T...) custom-call(s32[64]{0:T(128)} %counts_ref.1, ...), custom_call_target="tpu_custom_call" | custom-call | tf_op jit(solution)/shard_map/pallas_call | solution.py:395
  140.2 0.0 copy-start
  140.2 2.0 %copy.16 = bf16[128,2048]{1,0:T(8,128)(2,1)} copy(bf16[128,2048]{1,0:T(8,128)(2,1)} %get-tuple-element.12) | data formatting | bytes 1048576
  142.2 1.9 %copy.17 = bf16[128,2048]{1,0:T(8,128)(2,1)} copy(bf16[128,2048]{1,0:T(8,128)(2,1)} %get-tuple-element.13) | data formatting | bytes 1048576
  144.1 0.0 copy-done
  144.1 1.1 copy.18
Async XLA Ops:
  140.2 3.9 %copy-start = (bf16[2,768,512]{2,1,0:T(8,128)(2,1)S(1)}, bf16[2,768,512]{2,1,0:T(8,128)(2,1)}, u32[]{:S(2)}) copy-start(bf16[2,768,512]{2,1,0:T(8,128)(2,1)} %get-tuple-element.14) | copy-start | bytes 4718596
where the time goes:
time: 145 us
  Pallas kernels  140 us (97%)
  local copies, waits for them, and re-layouts  5.03 us (3%)
    pallas_call x1, Pallas kernels, on_device(): pl.pallas_call(kernel, out_shape=[jax.ShapeDtypeStruct((tok_n, width), BF...  140 us
    unnamed x5, local copies, waits for them, and re-layouts  5.03 us

commit v1 on v0

--- a/solution.py
+++ b/solution.py
@@ -213,7 +213,7 @@
         lax.fori_loop(0, 4, sums, 0)
         if n == 0:
             pl.semaphore_wait(barrier, len(peers))
-        start(n, 0)
+            start(n, 0)
 
         def local(q, carry):
             cols = pl.ds(pl.multiple_of(q * quarter, quarter), quarter)
@@ -229,7 +229,7 @@
     head(0, member_b, inverse, tok_ref, mix_out, loc_out)
     head(1, weight_b, None, cot_ref, mix_in, loc_in)
     relay_on(0)
-    relay_on(1)
+    start(1, 0)
     sent(0, 0)
     for load in loads:
         load.wait()
@@ -258,6 +258,7 @@
         return carry
 
     lax.fori_loop(0, ff // step, forward, 0)
+    relay_on(1)
 
     def out_cols(q, carry):
         cols = pl.ds(pl.multiple_of(q * quarter, quarter), quarter)
@@ -378,6 +379,21 @@
     for i in range(6):
         y_copy(i).wait_send()
     down_out.wait()
+
+
+def ship(*refs):
+    count = (len(refs) - 2) // 3
+    srcs, dsts, bufs = (refs[i * count:(i + 1) * count] for i in range(3))
+    in_sem, out_sem = refs[3 * count:]
+    reads = [pltpu.make_async_copy(s, b, in_sem.at[i]) for i, (s, b) in enumerate(zip(srcs, bufs))]
+    writes = [pltpu.make_async_copy(b, d, out_sem.at[i]) for i, (b, d) in enumerate(zip(bufs, dsts))]
+    for read in reads:
+        read.start()
+    for read, write in zip(reads, writes):
+        read.wait()
+        write.start()
+    for write in writes:
+        write.wait()
 
 
 def on_device(
@@ -428,7 +444,14 @@
         counts, expert_ids.T, bucket_codes.T, route_weights.T, tokens, cotangent, comp_scale,
         w_gate, w_up, w_down.reshape(local * ff, width),
     )
-    return tuple(out[:3])
+    shapes = [jax.ShapeDtypeStruct(a.shape, a.dtype) for a in out[:3]]
+    return tuple(pl.pallas_call(
+        ship,
+        out_shape=shapes,
+        in_specs=[hbm] * 3,
+        out_specs=[hbm] * 3,
+        scratch_shapes=[pltpu.VMEM(a.shape, a.dtype) for a in shapes] + [dma((3,)), dma((3,))],
+    )(*out[:3]))
 
 
 def solution(mesh):

time: 145 us -> 146 us (level)
  local copies, waits for them, and re-layouts: 5.03 us -> 0 us
  Pallas kernels: 140 us -> 145 us
    unnamed x5 -> x0, local copies, waits for them, and re-layouts: 5.03 us -> none
    pallas_call x0 -> x1, Pallas kernels: none -> 2.93 us  [on_device(): pl.pallas_call(ship, out_shape=shapes, in_specs=[hbm] * 3, out_specs=[hbm...]
    pallas_call x1, Pallas kernels: 140 us -> 142 us  [on_device(): pl.pallas_call(kernel, out_shape=[jax.ShapeDtypeStruct((tok_n, width), BF...]
where the time goes in v1:
time: 146 us; the launch traced here: 145 us
  Pallas kernels  145 us (99%)
    pallas_call x1, Pallas kernels, on_device(): pl.pallas_call(kernel, out_shape=[jax.ShapeDtypeStruct((tok_n, width), BF...  142 us
    pallas_call x1, Pallas kernels, on_device(): pl.pallas_call(ship, out_shape=shapes, in_specs=[hbm] * 3, out_specs=[hbm...  2.93 us

profile of v1, /device:TPU:1, one launch (start us, length us, event | category | flops | bytes accessed | tf_op | source)
XLA Modules:
  0.0 145.3 jit_solution(7316493616733223898)
XLA Ops:
  0.6 141.7 %shard_map.121 = (bf16[128,2048]{1,0:T(8,128)(2,1)}, bf16[128,2048]{1,0:T(8,128)(2,1)}, bf16[2,768,512]{2,1,0:T(8,128)(2,1)}, bf16[4,2,4,2,80,128]{5,4,3,2,1,0:T...) custom-call(s32[64]{0:T(128)} %counts_ref.1, ...), custom_call_target="tpu_custom_call" | custom-call | tf_op jit(solution)/shard_map/pallas_call | solution.py:411
  142.3 2.9 %shard_map.122 = (bf16[128,2048]{1,0:T(8,128)(2,1)}, bf16[128,2048]{1,0:T(8,128)(2,1)}, bf16[2,768,512]{2,1,0:T(8,128)(2,1)}) custom-call(bf16[128,2048]{1,0:T(8,128)(2,1)} %get-tuple-element.6.refs_0_, bf16[128,2048]{1,0:T(8,128)(2,1)} %get-tuple-element.7.refs_1_, bf16[2,768,512]{2,1,0:T(8,128)(2,1)} %get-tuple-element.8.refs_2_), custom_call_target="tpu_custom_call" | custom-call | tf_op jit(solution)/shard_map/pallas_call | solution.py:448

commit v2 on v1

--- a/solution.py
+++ b/solution.py
@@ -26,7 +26,7 @@
 def kernel(
     counts_ref, ids_ref, codes_ref, route_ref, tok_ref, cot_ref, comp_ref, wg_hbm, wu_hbm, wd_hbm,
     layer_ref, grad_ref, down_hbm, mid_a0, mid_a1, mid_b0, mid_b1, mid_c0, mid_c1, mid_d0, mid_d1,
-    send_0, send_1, got_a, got_b, got_c, got_d, wg, wu, wd, rows, gate, up, hid, dgs, dus,
+    send_0, send_1, got_a, got_b, got_c, got_d, wg, wu, wd, rows, spread, gate, up, hid, dgs, dus,
     part, relay, final, mix_out, mix_in, loc_out, loc_in, wsem, osem, ss1, rs1, ss2, rs2, yss, yrs,
 ):
     devs = NZ * NX * NC
@@ -67,37 +67,31 @@
     mids = ((mid_a0, mid_a1), (mid_b0, mid_b1), (mid_c0, mid_c1), (mid_d0, mid_d1))
     gots = (got_a, got_b, got_c, got_d)
 
-    def copies(n, phase):
-        out = ([], [])
+    def move(n, phase, side, d, k, here):
         buf, (mid_x, mid_z), got = sends[n], mids[n], gots[n]
         ssem, rsem = ((ss1, rs1), (ss2, rs2))[phase]
-        for d in FAR:
-            for k in (1, 0):
-                cc = (c + k) % NC
-                xx, zz = (x + d) % NX, (z + d) % NZ
-                if phase == 0:
-                    moves = (
-                        (buf.at[cc, :, xx], mid_x.at[x, c], x_dev(d, k)),
-                        (buf.at[NC + cc, zz], mid_z.at[z, c], z_dev(d, k)),
-                    )
-                else:
-                    moves = (
-                        (mid_z.at[:, :, xx, cc], got.at[NC + c, :, x], x_dev(d, k)),
-                        (mid_x.at[:, :, zz, cc], got.at[c, z], z_dev(d, k)),
-                    )
-                for side, (src, dst, dev) in enumerate(moves):
-                    i = d * NC + k
-                    if d + k:
-                        out[side].append(functools.partial(
-                            pltpu.make_async_remote_copy, src_ref=src, dst_ref=dst,
-                            send_sem=ssem.at[n, side, i], recv_sem=rsem.at[n, side, i],
-                            device_id=dev, device_id_type=MESH,
-                        ))
-                    else:
-                        out[side].append(functools.partial(
-                            pltpu.make_async_copy, src, dst, rsem.at[n, side, i]
-                        ))
-        return out
+        cc, xx, zz = (c + k) % NC, (x + d) % NX, (z + d) % NZ
+        if phase == 0 and side == 0:
+            src, dst = buf.at[cc, :, xx], mid_x.at[x, c]
+        elif phase == 0:
+            src, dst = buf.at[NC + cc, zz], mid_z.at[z, c]
+        elif side == 0:
+            src, dst = mid_z.at[:, :, xx, cc], got.at[NC + c, :, x]
+        else:
+            src, dst = mid_x.at[:, :, zz, cc], got.at[c, z]
+        i = d * NC + k
+        if here:
+            return pltpu.make_async_copy(src, dst, rsem.at[n, side, i])
+        return pltpu.make_async_remote_copy(
+            src_ref=src, dst_ref=dst, send_sem=ssem.at[n, side, i], recv_sem=rsem.at[n, side, i],
+            device_id=(z_dev if side else x_dev)(d, k), device_id_type=MESH,
+        )
+
+    def copies(n, phase):
+        return [
+            [functools.partial(move, n, phase, side, d, k, d + k == 0) for d in FAR for k in (1, 0)]
+            for side in range(2)
+        ]
 
     def start(n, phase, sides=(0, 1)):
         both = copies(n, phase)
@@ -128,17 +122,37 @@
         j = lax.broadcasted_iota(jnp.int32, (rows_n, cols_n), 0 if flip else 1)
         return (j == (i // REST) * TOP + q * REST + i % REST).astype(F32).astype(BF16)
 
-    def put_rows(n, q, value):
+    def lanes(g):
+        return [pl.ds(pl.multiple_of(q * quarter + g * LANES, LANES), LANES) for q in range(4)]
+
+    def send_groups(n, value_of):
         buf = sends[n]
-        rest = dot(pick(q, top_rows, devs * REST, True), value[top_rows:])
-        line = lax.broadcasted_iota(jnp.int32, (top_rows, 1), 0) % TOP // REST
-        at_q = pl.ds(pl.multiple_of(q * TOP, TOP), TOP)
-        for g in range(4):
-            cut = slice(g * LANES, (g + 1) * LANES)
-            buf[g, :, :, :, at_q, :] = value[:top_rows, cut].reshape(NZ, NX, NC, TOP, LANES)
-            old = buf[g, :, :, :, 4 * TOP:, :].reshape(top_rows, LANES)
-            new = jnp.where(line == q, rest[:, cut], old.astype(F32)).astype(BF16)
-            buf[g, :, :, :, 4 * TOP:, :] = new.reshape(NZ, NX, NC, TOP, LANES)
+
+        def body(j, carry):
+            cc = (c + 1 - j) % NC
+            for side in range(2):
+                g = side * NC + cc
+                value = value_of(g)
+                cuts = [slice(q * LANES, (q + 1) * LANES) for q in range(4)]
+                for q in range(4):
+                    top = value[:top_rows, cuts[q]]
+                    buf[g, :, :, :, q * TOP:(q + 1) * TOP, :] = top.reshape(NZ, NX, NC, TOP, LANES)
+                rest = jnp.concatenate([value[top_rows:, cuts[q]] for q in range(4)], axis=0)
+                rest = dot(spread[...], rest).astype(BF16)
+                buf[g, :, :, :, 4 * TOP:, :] = rest.reshape(NZ, NX, NC, TOP, LANES)
+                for d in FAR[:3]:
+                    move(n, 0, side, d, 1 - j, False).start()
+
+                @pl.when(j == 0)
+                def _():
+                    move(n, 0, side, 0, 1, False).start()
+
+                @pl.when(j == 1)
+                def _():
+                    move(n, 0, side, 0, 0, True).start()
+            return carry
+
+        lax.fori_loop(0, NC, body, 0)
 
     def take_rows(n):
         got = gots[n]
@@ -200,20 +214,18 @@
     ).astype(BF16)
 
     def head(n, lhs, scale, src, mix, loc):
-        def sums(q, carry):
-            cols = pl.ds(pl.multiple_of(q * quarter, quarter), quarter)
-            value = dot(lhs, src[:, cols])
+        def sums(g):
+            value = dot(lhs, jnp.concatenate([src[:, cols] for cols in lanes(g)], axis=1))
             if scale is not None:
                 value = value * scale
             value = value.astype(BF16)
-            rows[:, cols] = value
-            put_rows(n, q, value)
-            return carry
-
-        lax.fori_loop(0, 4, sums, 0)
+            for q, cols in enumerate(lanes(g)):
+                rows[:, cols] = value[:, q * LANES:(q + 1) * LANES]
+            return value
+
         if n == 0:
             pl.semaphore_wait(barrier, len(peers))
-            start(n, 0)
+        send_groups(n, sums)
 
         def local(q, carry):
             cols = pl.ds(pl.multiple_of(q * quarter, quarter), quarter)
@@ -224,12 +236,14 @@
 
         lax.fori_loop(0, 4, local, 0)
 
-    for ref in (send_0, send_1):
-        ref[:, :, :, :, 4 * TOP:, :] = jnp.zeros((4, NZ, NX, NC, TOP, LANES), BF16)
+    to = lax.broadcasted_iota(jnp.int32, (top_rows, 4 * devs * REST), 0)
+    of = lax.broadcasted_iota(jnp.int32, (top_rows, 4 * devs * REST), 1)
+    put_at = to % TOP // REST * (devs * REST) + to // TOP * REST + to % REST
+    spread[...] = (of == put_at).astype(F32).astype(BF16)
     head(0, member_b, inverse, tok_ref, mix_out, loc_out)
     head(1, weight_b, None, cot_ref, mix_in, loc_in)
     relay_on(0)
-    start(1, 0)
+    relay_on(1)
     sent(0, 0)
     for load in loads:
         load.wait()
@@ -258,15 +272,12 @@
         return carry
 
     lax.fori_loop(0, ff // step, forward, 0)
-    relay_on(1)
-
-    def out_cols(q, carry):
-        cols = pl.ds(pl.multiple_of(q * quarter, quarter), quarter)
-        put_rows(2, q, dot(hid[...], wd[:, cols]).astype(BF16))
-        return carry
-
-    lax.fori_loop(0, 4, out_cols, 0)
-    start(2, 0)
+
+    def out_cols(g):
+        w = jnp.concatenate([wd[:, cols] for cols in lanes(g)], axis=1)
+        return dot(hid[...], w).astype(BF16)
+
+    send_groups(2, out_cols)
 
     arrive(1, 1)
     sent(1, 0)
@@ -319,18 +330,16 @@
     lax.fori_loop(0, ff // step, backward, 0)
     relay_on(2)
 
-    def back_cols(q, carry):
-        at_q = pl.ds(pl.multiple_of(q * quarter, quarter), quarter)
+    def back_cols(g):
         total = jnp.zeros((all_rows, quarter), F32)
         for e in range(2):
             half = slice(e * ff, (e + 1) * ff)
-            total += dot(dgs[:, half], wg[e, at_q, :], 1, 1)
-            total += dot(dus[:, half], wu[e, at_q, :], 1, 1)
-        put_rows(3, q, total.astype(BF16))
-        return carry
-
-    lax.fori_loop(0, 4, back_cols, 0)
-    start(3, 0)
+            for ref, w in ((dgs, wg), (dus, wu)):
+                side = jnp.concatenate([w[e, cols, :] for cols in lanes(g)], axis=0)
+                total += dot(ref[:, half], side, 1, 1)
+        return total.astype(BF16)
+
+    send_groups(3, back_cols)
 
     for i, shift, e in ((0, 1, 0), (1, NY - 1, 1)):
         y_copy(i).wait_recv()
@@ -422,6 +431,7 @@
             pltpu.VMEM((local, width, ff), BF16),
             pltpu.VMEM((local * ff, width), BF16),
             pltpu.VMEM((all_rows, width), BF16),
+            pltpu.VMEM((devs * TOP, 4 * devs * REST), BF16),
             pltpu.VMEM((all_rows, ff), BF16),
             pltpu.VMEM((all_rows, ff), BF16),
             pltpu.VMEM((all_rows, local * ff), BF16),

time: 146 us -> 142 us (0.973)
  Pallas kernels: 145 us -> 141 us
    pallas_call x1, Pallas kernels: 142 us -> 138 us  [on_device(): pl.pallas_call(kernel, out_shape=[jax.ShapeDtypeStruct((tok_n, width), BF...]
where the time goes in v2:
time: 142 us
  Pallas kernels  141 us (99%)
    pallas_call x1, Pallas kernels, on_device(): pl.pallas_call(kernel, out_shape=[jax.ShapeDtypeStruct((tok_n, width), BF...  138 us
    pallas_call x1, Pallas kernels, on_device(): pl.pallas_call(ship, out_shape=shapes, in_specs=[hbm] * 3, out_specs=[hbm...  2.93 us

profile of v2, /device:TPU:1, one launch (start us, length us, event | category | flops | bytes accessed | tf_op | source)
XLA Modules:
  0.0 142.0 jit_solution(14917839725039141129)
XLA Ops:
  0.6 138.3 %shard_map.121 = (bf16[128,2048]{1,0:T(8,128)(2,1)}, bf16[128,2048]{1,0:T(8,128)(2,1)}, bf16[2,768,512]{2,1,0:T(8,128)(2,1)}, bf16[4,2,4,2,80,128]{5,4,3,2,1,0:T...) custom-call(s32[64]{0:T(128)} %counts_ref.1, ...), custom_call_target="tpu_custom_call" | custom-call | tf_op jit(solution)/shard_map/pallas_call | solution.py:420
  138.9 2.9 %shard_map.122 = (bf16[128,2048]{1,0:T(8,128)(2,1)}, bf16[128,2048]{1,0:T(8,128)(2,1)}, bf16[2,768,512]{2,1,0:T(8,128)(2,1)}) custom-call(bf16[128,2048]{1,0:T(8,128)(2,1)} %get-tuple-element.6.refs_0_, bf16[128,2048]{1,0:T(8,128)(2,1)} %get-tuple-element.7.refs_1_, bf16[2,768,512]{2,1,0:T(8,128)(2,1)} %get-tuple-element.8.refs_2_), custom_call_target="tpu_custom_call" | custom-call | tf_op jit(solution)/shard_map/pallas_call | solution.py:458

commit v3 on v2

--- a/solution.py
+++ b/solution.py
@@ -314,7 +314,6 @@
     y_copy(2).start()
     down(NY - 1)
     y_copy(3).start()
-    down(0)
 
     def backward(i, carry):
         f = pl.multiple_of(i * step, step)
@@ -340,6 +339,7 @@
         return total.astype(BF16)
 
     send_groups(3, back_cols)
+    down(0)
 
     for i, shift, e in ((0, 1, 0), (1, NY - 1, 1)):
         y_copy(i).wait_recv()

time: 142 us -> 140 us (0.986)
  Pallas kernels: 141 us -> 139 us
    pallas_call x1, Pallas kernels: 138 us -> 136 us  [on_device(): pl.pallas_call(kernel, out_shape=[jax.ShapeDtypeStruct((tok_n, width), BF...]
where the time goes in v3:
time: 140 us
  Pallas kernels  139 us (99%)
    pallas_call x1, Pallas kernels, on_device(): pl.pallas_call(kernel, out_shape=[jax.ShapeDtypeStruct((tok_n, width), BF...  136 us
    pallas_call x1, Pallas kernels, on_device(): pl.pallas_call(ship, out_shape=shapes, in_specs=[hbm] * 3, out_specs=[hbm...  2.93 us

profile of v3, /device:TPU:1, one launch (start us, length us, event | category | flops | bytes accessed | tf_op | source)
XLA Modules:
  0.0 140.2 jit_solution(10467117785835735592)
XLA Ops:
  0.6 136.5 %shard_map.121 = (bf16[128,2048]{1,0:T(8,128)(2,1)}, bf16[128,2048]{1,0:T(8,128)(2,1)}, bf16[2,768,512]{2,1,0:T(8,128)(2,1)}, bf16[4,2,4,2,80,128]{5,4,3,2,1,0:T...) custom-call(s32[64]{0:T(128)} %counts_ref.1, ...), custom_call_target="tpu_custom_call" | custom-call | tf_op jit(solution)/shard_map/pallas_call | solution.py:420
  137.1 2.9 %shard_map.122 = (bf16[128,2048]{1,0:T(8,128)(2,1)}, bf16[128,2048]{1,0:T(8,128)(2,1)}, bf16[2,768,512]{2,1,0:T(8,128)(2,1)}) custom-call(bf16[128,2048]{1,0:T(8,128)(2,1)} %get-tuple-element.6.refs_0_, bf16[128,2048]{1,0:T(8,128)(2,1)} %get-tuple-element.7.refs_1_, bf16[2,768,512]{2,1,0:T(8,128)(2,1)} %get-tuple-element.8.refs_2_), custom_call_target="tpu_custom_call" | custom-call | tf_op jit(solution)/shard_map/pallas_call | solution.py:458
